TPU v7x, 256 devices: a whole 4x4x8 slice. The times are simulated.
256 devices in a mesh: slab: 64 (over z_lo, x, y), probe: 4 (over z_hi, core).
Axes of the slice: x: 4, y: 4, z: 8 (z_hi: 2, z_lo: 4; z = z_hi * 4 + z_lo), core: 2. Of those that a mesh axis runs over, the one named last changes fastest.
Arguments:
- probes: int32 [4, 32, 1024, 512], P('probe', None, 'slab'), may hold values 0 or 1
- snapshots: float32 [4, 32, 1024, 512], P('probe', None, 'slab'), may hold values from -16 to 16
- kappa: float32 [32, 1024, 512], P(None, 'slab'), may hold values from 0.05 to 0.18
Outputs:
- precond: float32 [32, 1024, 512], P(None, 'slab', 'probe')
All inputs are finite; a program needn't handle non-finite values. No bound on the sum of `probes` on one device may be relied on, other than what follows from the above.
Results may differ from a plain program's by a relative error of at most 0.00017.
Values sent between devices are 32-bit elements; how exact they have to be, the bound alone decides.
No kernel may reach another device: no remote copies, remote signals or barrier semaphores. Data moves between devices by JAX's collectives and lax.ppermute only.
A program may use at most 64 MiB of HBM per device.

v0:
```python
import jax
import jax.numpy as jnp
from jax import lax
from jax.sharding import PartitionSpec as P

NT = 4


COEFFS = (-205.0 / 72.0, 8.0 / 5.0, -1.0 / 5.0, 8.0 / 315.0, -1.0 / 560.0)
EPSILON = 1e-06


def extended_2(cells, sides, width):
    for axis, dim in sides:
        count = lax.axis_size(axis)
        ends = count - 1
        head = lax.slice_in_dim(cells, 0, width, axis=dim)
        tail = lax.slice_in_dim(cells, cells.shape[dim] - width, cells.shape[dim], axis=dim)
        cells = jnp.concatenate(
            [
                lax.ppermute(tail, axis, [(i, (i + 1) % count) for i in range(ends)]),
                cells,
                lax.ppermute(head, axis, [((i + 1) % count, i) for i in range(ends)]),
            ],
            axis=dim,
        )
    return cells


def stencil(padded, n_depth, n_rows, n_width):
    centre = padded[:, 4 : 4 + n_depth, 4 : 4 + n_rows, 4 : 4 + n_width]
    summed = 3.0 * COEFFS[0] * centre
    for offset in range(1, 5):
        paired = padded[:, 4 + offset : 4 + offset + n_depth, 4 : 4 + n_rows, 4 : 4 + n_width]
        paired = (
            paired + padded[:, 4 - offset : 4 - offset + n_depth, 4 : 4 + n_rows, 4 : 4 + n_width]
        )
        paired = (
            paired + padded[:, 4 : 4 + n_depth, 4 + offset : 4 + offset + n_rows, 4 : 4 + n_width]
        )
        paired = (
            paired + padded[:, 4 : 4 + n_depth, 4 - offset : 4 - offset + n_rows, 4 : 4 + n_width]
        )
        paired = (
            paired + padded[:, 4 : 4 + n_depth, 4 : 4 + n_rows, 4 + offset : 4 + offset + n_width]
        )
        paired = (
            paired + padded[:, 4 : 4 + n_depth, 4 : 4 + n_rows, 4 - offset : 4 - offset + n_width]
        )
        summed = summed + COEFFS[offset] * paired
    return summed


def laplace(field):
    extended = extended_2(field, (("slab", 2),), 4)
    padded = jnp.pad(extended, ((0, 0), (4, 4), (0, 0), (4, 4)))
    return stencil(padded, field.shape[1], field.shape[2], field.shape[3])


def body(probes, snapshots, kappa):
    signs = (2 * probes - 1).astype(jnp.float32)
    coeff_field = kappa[None]
    gathered = lax.all_gather(snapshots, "probe", axis=0, tiled=True)
    frames = [gathered[moment] for moment in range(NT)]
    previous = jnp.zeros_like(signs)
    current = signs * frames[0][None]
    scattered = [current]
    for moment in range(1, NT):
        following = (
            2.0 * current - previous + coeff_field * laplace(current) + signs * frames[moment][None]
        )
        previous = current
        current = following
        scattered.append(current)
    later = jnp.zeros_like(signs)
    adjoint = scattered[NT - 1]
    image = frames[NT - 1][None] * adjoint
    for moment in range(NT - 2, -1, -1):
        earlier = scattered[moment] + 2.0 * adjoint - later + laplace(coeff_field * adjoint)
        later = adjoint
        adjoint = earlier
        image = image + frames[moment][None] * adjoint
    estimate = jnp.sum(signs * image, axis=0)
    cell_count = estimate.size * lax.axis_size("slab")
    share = lax.psum_scatter(estimate, "probe", scatter_dimension=2, tiled=True)
    squares = lax.psum(jnp.sum(share * share), ("slab", "probe"))
    return share / jnp.sqrt(squares / cell_count + EPSILON)


def solution(mesh):
    return jax.shard_map(
        body,
        mesh=mesh,
        in_specs=(
            P("probe", None, "slab", None),
            P("probe", None, "slab", None),
            P(None, "slab", None),
        ),
        out_specs=P(None, "slab", "probe"),
        check_vma=False,
    )
```

profile of v0, /device:TPU:1, one launch (start us, length us, event | category | flops | bytes accessed | tf_op | source)
XLA Modules:
  0.0 382.3 jit_solution(10218467963391972248)
XLA Ops:
  6.5 0.0 all-gather.2.cloned.1.call-start
  6.5 0.7 all-gather.2.cloned.1.call-update
  7.3 0.0 reduce-scatter.2.cloned.1.call-start
  7.3 72.6 %all-gather.2.cloned.1.call-done = f32[4,32,16,512]{3,2,1,0:T(8,128)} async-done(((f32[1,32,16,512]{3,2,1,0:T(8,128)}), f32[4,32,16,512]{3,2,1,0:T(8,128)}) %all-gather.2.cloned.1.call-update) | async-done | bytes 4194320 | tf_op jit(solution)/shard_map/all_gather | solution.py:63
  79.9 1.8 convert_multiply_fusion
  81.7 0.0 copy-start
  81.7 0.0 copy-start.1
  81.7 0.1 fusion.195
  81.8 1.4 collective-permute-start.1
  83.2 4.0 %collective-permute-start = (f32[1,32,4,512]{3,2,1,0:T(4,128)S(1)}, f32[1,32,4,512]{3,2,1,0:T(4,128)S(1)}, u32[]{:S(2)}, u32[]{:S(2)}) collective-permute-start(f32[1,32,4,512]{3,2,1,0:T(4,128)S(1)} %get-tuple-element.22), channel_id=1, source_target_pairs={{0,4},{4,8},{8,12},{12,16},{16,20},{20,24},{24,28},{28,32},{32,36}... | collective-permute-start | bytes 786440 | tf_op jit(solution)/shard_map/ppermute | solution.py:21
  87.2 4.2 %collective-permute-done.1 = f32[1,32,4,512]{3,2,1,0:T(4,128)S(1)} collective-permute-done((f32[1,32,4,512]{3,2,1,0:T(4,128)S(1)}, f32[1,32,4,512]{3,2,1,0:T(4,128)S(1)}, u32[]{:S(2)}, u32[]{:S(2)}) %collective-permute-start.1) | collective-permute-done | bytes 262176 | tf_op jit(solution)/shard_map/ppermute | solution.py:23
  91.4 0.9 collective-permute-done
  92.3 1.1 select_maximum_fusion.10
  93.4 0.0 copy-done
  93.4 0.0 copy-done.1
  93.4 6.0 %fusion.150 = f32[1,32,16,512]{3,2,1,0:T(8,128)S(1)} fusion(f32[1,32,16,512]{3,2,1,0:T(8,128)S(1)} %convert_multiply_fusion, f32[1,32,4,512]{3,2,1,0:T(4,128)S(1)} %collective-permute-done, f32[1,32,4,512]{3,2,1,0:T(4,128)S(1)} %collective-permute-done.1, f32[1,40,24,520]{3,2,1,0:T(8,128)S(1)} %select_maximum_fusion.10, f32[32,16,512]{2,1,0:T(8,128)S(1)} %copy-done, ...), kind=kLoop, calls=%fused_computation.238 | loop fusion | flops 11796480 | bytes 22544384 | tf_op jit(solution)/shard_map/add | solution.py:70
  99.4 0.0 copy-start.2
  99.4 0.1 fusion.194
  99.5 1.4 collective-permute-start.3
  101.0 4.7 %collective-permute-start.2 = (f32[1,32,4,512]{3,2,1,0:T(4,128)S(1)}, f32[1,32,4,512]{3,2,1,0:T(4,128)S(1)}, u32[]{:S(2)}, u32[]{:S(2)}) collective-permute-start(f32[1,32,4,512]{3,2,1,0:T(4,128)S(1)} %get-tuple-element.20), channel_id=1, source_target_pairs={{0,4},{4,8},{8,12},{12,16},{16,20},{20,24},{24,28},{28,32},{32,36}... | collective-permute-start | bytes 786440 | tf_op jit(solution)/shard_map/ppermute | solution.py:21
  105.7 3.3 collective-permute-done.3
  109.0 0.9 collective-permute-done.2
  109.9 1.1 select_maximum_fusion.8
  111.0 0.0 copy-done.2
  111.0 6.9 %fusion.122 = f32[1,32,16,512]{3,2,1,0:T(8,128)} fusion(f32[1,32,16,512]{3,2,1,0:T(8,128)S(1)} %fusion.150, f32[1,32,4,512]{3,2,1,0:T(4,128)S(1)} %collective-permute-done.2, f32[1,32,4,512]{3,2,1,0:T(4,128)S(1)} %collective-permute-done.3, f32[1,40,24,520]{3,2,1,0:T(8,128)S(1)} %select_maximum_fusion.8, f32[32,16,512]{2,1,0:T(8,128)S(1)} %copy-done, ...), kind=kLoop, calls=%fused_computation.210 | loop fusion | flops 12320768 | bytes 23592960 | tf_op jit(solution)/shard_map/add | solution.py:70
  117.9 1.3 fusion.193
  119.2 4.1 %collective-permute-start.4 = (f32[1,32,4,512]{3,2,1,0:T(4,128)S(1)}, f32[1,32,4,512]{3,2,1,0:T(4,128)S(1)}, u32[]{:S(2)}, u32[]{:S(2)}) collective-permute-start(f32[1,32,4,512]{3,2,1,0:T(4,128)S(1)} %get-tuple-element.17), channel_id=1, source_target_pairs={{0,4},{4,8},{8,12},{12,16},{16,20},{20,24},{24,28},{28,32},{32,36}... | collective-permute-start | bytes 786440 | tf_op jit(solution)/shard_map/ppermute | solution.py:21
  123.3 1.5 collective-permute-start.5
  124.8 1.8 collective-permute-done.4
  126.6 3.8 %collective-permute-done.5 = f32[1,32,4,512]{3,2,1,0:T(4,128)S(1)} collective-permute-done((f32[1,32,4,512]{3,2,1,0:T(4,128)S(1)}, f32[1,32,4,512]{3,2,1,0:T(4,128)S(1)}, u32[]{:S(2)}, u32[]{:S(2)}) %collective-permute-start.5) | collective-permute-done | bytes 262176 | tf_op jit(solution)/shard_map/ppermute | solution.py:23
  130.5 2.3 select_maximum_fusion.6
  132.8 11.2 %bitcast_multiply_fusion.2 = (f32[1,32,16,512]{3,2,1,0:T(8,128)}, f32[1,32,16,512]{3,2,1,0:T(8,128)}) fusion(f32[32,16,512]{2,1,0:T(8,128)S(1)} %copy-done, f32[4,32,16,512]{3,2,1,0:T(8,128)} %all-gather.2.cloned.1.call-done, s32[1,32,16,512]{3,2,1,0:T(8,128)} %param.3, f32[1,40,24,520]{3,2,1,0:T(8,128)S(1)} %select_maximum_fusion.6, ...), kind=kLoop, calls=%fused_computation.325 | loop fusion | flops 12320768 | bytes 24641536 | tf_op jit(solution)/shard_map/mul | solution.py:79
  144.0 0.0 copy-start.4
  144.0 1.4 fusion.192
  145.4 6.2 %collective-permute-start.6 = (f32[1,32,4,512]{3,2,1,0:T(4,128)S(1)}, f32[1,32,4,512]{3,2,1,0:T(4,128)S(1)}, u32[]{:S(2)}, u32[]{:S(2)}) collective-permute-start(f32[1,32,4,512]{3,2,1,0:T(4,128)S(1)} %get-tuple-element.15), channel_id=1, source_target_pairs={{0,4},{4,8},{8,12},{12,16},{16,20},{20,24},{24,28},{28,32},{32,36}... | collective-permute-start | bytes 786440 | tf_op jit(solution)/shard_map/ppermute | solution.py:21
  151.6 1.3 collective-permute-start.7
  152.9 2.0 collective-permute-done.6
  154.9 6.7 %collective-permute-done.7 = f32[1,32,4,512]{3,2,1,0:T(4,128)S(1)} collective-permute-done((f32[1,32,4,512]{3,2,1,0:T(4,128)S(1)}, f32[1,32,4,512]{3,2,1,0:T(4,128)S(1)}, u32[]{:S(2)}, u32[]{:S(2)}) %collective-permute-start.7) | collective-permute-done | bytes 262176 | tf_op jit(solution)/shard_map/ppermute | solution.py:23
  161.5 2.3 select_maximum_fusion.4
  163.8 0.0 copy-done.4
  163.8 11.2 %bitcast_multiply_fusion.1 = (f32[1,32,16,512]{3,2,1,0:T(8,128)}, f32[1,32,16,512]{3,2,1,0:T(8,128)}) fusion(f32[32,16,512]{2,1,0:T(8,128)S(1)} %copy-done, f32[1,40,24,520]{3,2,1,0:T(8,128)S(1)} %select_maximum_fusion.4, f32[1,32,16,512]{3,2,1,0:T(8,128)} %get-tuple-element.9, f32[1,32,4,512]{3,2,1,0:T(4,128)S(1)} %collective-permute-done.6, ...), kind=kLoop, calls=%fused_computation.324 | loop fusion | flops 10747904 | bytes 23592960 | tf_op jit(solution)/shard_map/mul | solution.py:79
  175.0 1.3 fusion.191
  176.3 5.1 %collective-permute-start.8 = (f32[1,32,4,512]{3,2,1,0:T(4,128)S(1)}, f32[1,32,4,512]{3,2,1,0:T(4,128)S(1)}, u32[]{:S(2)}, u32[]{:S(2)}) collective-permute-start(f32[1,32,4,512]{3,2,1,0:T(4,128)S(1)} %get-tuple-element.13), channel_id=1, source_target_pairs={{0,4},{4,8},{8,12},{12,16},{16,20},{20,24},{24,28},{28,32},{32,36}... | collective-permute-start | bytes 786440 | tf_op jit(solution)/shard_map/ppermute | solution.py:21
  181.5 1.3 collective-permute-start.9
  182.8 2.0 collective-permute-done.8
  184.7 3.8 %collective-permute-done.9 = f32[1,32,4,512]{3,2,1,0:T(4,128)S(1)} collective-permute-done((f32[1,32,4,512]{3,2,1,0:T(4,128)S(1)}, f32[1,32,4,512]{3,2,1,0:T(4,128)S(1)}, u32[]{:S(2)}, u32[]{:S(2)}) %collective-permute-start.9) | collective-permute-done | bytes 262176 | tf_op jit(solution)/shard_map/ppermute | solution.py:23
  188.6 2.3 select_maximum_fusion.2
  190.9 11.5 %bitcast_multiply_fusion = (f32[1,32,16,512]{3,2,1,0:T(8,128)}, f32[1,32,16,512]{3,2,1,0:T(8,128)}) fusion(f32[32,16,512]{2,1,0:T(8,128)S(1)} %copy-done, f32[1,40,24,520]{3,2,1,0:T(8,128)S(1)} %select_maximum_fusion.2, f32[1,32,16,512]{3,2,1,0:T(8,128)} %get-tuple-element.7, f32[1,32,4,512]{3,2,1,0:T(4,128)S(1)} %collective-permute-done.8, ...), kind=kLoop, calls=%fused_computation.323 | loop fusion | flops 11010048 | bytes 24641536 | tf_op jit(solution)/shard_map/mul | solution.py:79
  202.4 0.0 copy-start.3
  202.4 1.4 fusion.190
  203.8 1.3 collective-permute-start.11
  205.1 5.2 %collective-permute-start.10 = (f32[1,32,4,512]{3,2,1,0:T(4,128)S(1)}, f32[1,32,4,512]{3,2,1,0:T(4,128)S(1)}, u32[]{:S(2)}, u32[]{:S(2)}) collective-permute-start(f32[1,32,4,512]{3,2,1,0:T(4,128)S(1)} %get-tuple-element.12), channel_id=1, source_target_pairs={{0,4},{4,8},{8,12},{12,16},{16,20},{20,24},{24,28},{28,32},{32,36}... | collective-permute-start | bytes 786440 | tf_op jit(solution)/shard_map/ppermute | solution.py:21
  210.3 1.6 collective-permute-done.11
  211.9 1.5 collective-permute-done.10
  213.3 0.0 copy-done.5
  213.3 2.4 select_maximum_fusion
  215.7 0.0 copy-done.6
  215.7 0.0 copy-done.3
  215.7 13.2 %fusion.14 = f32[32,16,512]{2,1,0:T(8,128)} fusion(f32[1,32,16,512]{3,2,1,0:T(8,128)} %get-tuple-element.5, f32[1,32,4,512]{3,2,1,0:T(4,128)} %copy-done.6, f32[1,32,4,512]{3,2,1,0:T(4,128)} %copy-done.5, f32[1,40,24,520]{3,2,1,0:T(8,128)S(1)} %select_maximum_fusion, f32[1,32,16,512]{3,2,1,0:T(8,128)} %get-tuple-element.8, ...), kind=kLoop, calls=%fused_computation.102 | loop fusion | flops 13893632 | bytes 27787264 | tf_op jit(solution)/shard_map/reduce_sum | solution.py:83
  228.9 0.0 reduce-scatter.2.cloned.1.call-update
  229.0 67.4 %reduce-scatter.2.cloned.1.call-done = f32[32,16,128]{2,1,0:T(8,128)} async-done(((f32[32,16,512]{2,1,0:T(8,128)}), f32[32,16,128]{2,1,0:T(8,128)}) %reduce-scatter.2.cloned.1.call-update) | async-done | bytes 262160 | tf_op jit(solution)/shard_map/reduce_scatter | solution.py:85
  296.4 1.6 multiply_reduce_fusion
  298.0 75.1 %psum.7 = f32[]{:T(128)} all-reduce(f32[]{:T(128)} %multiply_reduce_fusion), channel_id=1, replica_groups=mesh['slab'=64,'probe'=4] {'slab','probe'}, use_global_device_ids=true, to_apply=%region_2.3 | all-reduce | flops 1 | bytes 8 | tf_op jit(solution)/shard_map/psum | solution.py:86
  373.8 1.7 broadcast_divide_fusion
  (2 shorter events, 0.0 us)
Async XLA Ops:
  6.5 73.3 %all-gather.2.cloned.1.call-start = ((), (), s32[]{:S(2)}) async-start(), calls=%async_computation.1 | async-start | bytes 5242880 | tf_op jit(solution)/shard_map/all_gather | solution.py:63
  7.3 289.1 %reduce-scatter.2.cloned.1.call-start = ((), (), s32[]{:S(2)}) async-start(), calls=%async_computation.2 | async-start | bytes 1310720 | tf_op jit(solution)/shard_map/reduce_scatter | solution.py:85
  81.7 11.7 %copy-start = (f32[32,16,512]{2,1,0:T(8,128)S(1)}, f32[32,16,512]{2,1,0:T(8,128)}, u32[]{:S(2)}) copy-start(f32[32,16,512]{2,1,0:T(8,128)} %param.5) | copy-start | bytes 3145732
  81.7 11.7 %copy-start.1 = (s32[1,32,16,512]{3,2,1,0:T(8,128)S(1)}, s32[1,32,16,512]{3,2,1,0:T(8,128)}, u32[]{:S(2)}) copy-start(s32[1,32,16,512]{3,2,1,0:T(8,128)} %param.3) | copy-start | bytes 3145732
  81.8 9.6 %collective-permute-start.1 = (f32[1,32,4,512]{3,2,1,0:T(4,128)S(1)}, f32[1,32,4,512]{3,2,1,0:T(4,128)S(1)}, u32[]{:S(2)}, u32[]{:S(2)}) collective-permute-start(f32[1,32,4,512]{3,2,1,0:T(4,128)S(1)} %get-tuple-element.21), channel_id=1, source_target_pairs={{4,0},{8,4},{12,8},{16,12},{20,16},{24,20},{28,24},{32,28},{36,32}... | collective-permute-start | bytes 786440 | tf_op jit(solution)/shard_map/ppermute | solution.py:23
  83.2 9.1 %collective-permute-start = (f32[1,32,4,512]{3,2,1,0:T(4,128)S(1)}, f32[1,32,4,512]{3,2,1,0:T(4,128)S(1)}, u32[]{:S(2)}, u32[]{:S(2)}) collective-permute-start(f32[1,32,4,512]{3,2,1,0:T(4,128)S(1)} %get-tuple-element.22), channel_id=1, source_target_pairs={{0,4},{4,8},{8,12},{12,16},{16,20},{20,24},{24,28},{28,32},{32,36}... | collective-permute-start | bytes 786440 | tf_op jit(solution)/shard_map/ppermute | solution.py:21
  99.4 11.6 %copy-start.2 = (s32[1,32,16,512]{3,2,1,0:T(8,128)S(1)}, s32[1,32,16,512]{3,2,1,0:T(8,128)}, u32[]{:S(2)}) copy-start(s32[1,32,16,512]{3,2,1,0:T(8,128)} %param.3) | copy-start | bytes 3145732
  99.5 9.5 %collective-permute-start.3 = (f32[1,32,4,512]{3,2,1,0:T(4,128)S(1)}, f32[1,32,4,512]{3,2,1,0:T(4,128)S(1)}, u32[]{:S(2)}, u32[]{:S(2)}) collective-permute-start(f32[1,32,4,512]{3,2,1,0:T(4,128)S(1)} %get-tuple-element.19), channel_id=1, source_target_pairs={{4,0},{8,4},{12,8},{16,12},{20,16},{24,20},{28,24},{32,28},{36,32}... | collective-permute-start | bytes 786440 | tf_op jit(solution)/shard_map/ppermute | solution.py:23
  101.0 9.0 %collective-permute-start.2 = (f32[1,32,4,512]{3,2,1,0:T(4,128)S(1)}, f32[1,32,4,512]{3,2,1,0:T(4,128)S(1)}, u32[]{:S(2)}, u32[]{:S(2)}) collective-permute-start(f32[1,32,4,512]{3,2,1,0:T(4,128)S(1)} %get-tuple-element.20), channel_id=1, source_target_pairs={{0,4},{4,8},{8,12},{12,16},{16,20},{20,24},{24,28},{28,32},{32,36}... | collective-permute-start | bytes 786440 | tf_op jit(solution)/shard_map/ppermute | solution.py:21
  119.2 7.4 %collective-permute-start.4 = (f32[1,32,4,512]{3,2,1,0:T(4,128)S(1)}, f32[1,32,4,512]{3,2,1,0:T(4,128)S(1)}, u32[]{:S(2)}, u32[]{:S(2)}) collective-permute-start(f32[1,32,4,512]{3,2,1,0:T(4,128)S(1)} %get-tuple-element.17), channel_id=1, source_target_pairs={{0,4},{4,8},{8,12},{12,16},{16,20},{20,24},{24,28},{28,32},{32,36}... | collective-permute-start | bytes 786440 | tf_op jit(solution)/shard_map/ppermute | solution.py:21
  123.3 7.1 %collective-permute-start.5 = (f32[1,32,4,512]{3,2,1,0:T(4,128)S(1)}, f32[1,32,4,512]{3,2,1,0:T(4,128)S(1)}, u32[]{:S(2)}, u32[]{:S(2)}) collective-permute-start(f32[1,32,4,512]{3,2,1,0:T(4,128)S(1)} %get-tuple-element.18), channel_id=1, source_target_pairs={{4,0},{8,4},{12,8},{16,12},{20,16},{24,20},{28,24},{32,28},{36,32}... | collective-permute-start | bytes 786440 | tf_op jit(solution)/shard_map/ppermute | solution.py:23
  144.0 19.8 %copy-start.4 = (f32[1,32,16,512]{3,2,1,0:T(8,128)S(1)}, f32[1,32,16,512]{3,2,1,0:T(8,128)}, u32[]{:S(2)}) copy-start(f32[1,32,16,512]{3,2,1,0:T(8,128)} %fusion.122) | copy-start | bytes 3145732
  145.4 9.5 %collective-permute-start.6 = (f32[1,32,4,512]{3,2,1,0:T(4,128)S(1)}, f32[1,32,4,512]{3,2,1,0:T(4,128)S(1)}, u32[]{:S(2)}, u32[]{:S(2)}) collective-permute-start(f32[1,32,4,512]{3,2,1,0:T(4,128)S(1)} %get-tuple-element.15), channel_id=1, source_target_pairs={{0,4},{4,8},{8,12},{12,16},{16,20},{20,24},{24,28},{28,32},{32,36}... | collective-permute-start | bytes 786440 | tf_op jit(solution)/shard_map/ppermute | solution.py:21
  151.6 10.0 %collective-permute-start.7 = (f32[1,32,4,512]{3,2,1,0:T(4,128)S(1)}, f32[1,32,4,512]{3,2,1,0:T(4,128)S(1)}, u32[]{:S(2)}, u32[]{:S(2)}) collective-permute-start(f32[1,32,4,512]{3,2,1,0:T(4,128)S(1)} %get-tuple-element.16), channel_id=1, source_target_pairs={{4,0},{8,4},{12,8},{16,12},{20,16},{24,20},{28,24},{32,28},{36,32}... | collective-permute-start | bytes 786440 | tf_op jit(solution)/shard_map/ppermute | solution.py:23
  176.3 8.4 %collective-permute-start.8 = (f32[1,32,4,512]{3,2,1,0:T(4,128)S(1)}, f32[1,32,4,512]{3,2,1,0:T(4,128)S(1)}, u32[]{:S(2)}, u32[]{:S(2)}) collective-permute-start(f32[1,32,4,512]{3,2,1,0:T(4,128)S(1)} %get-tuple-element.13), channel_id=1, source_target_pairs={{0,4},{4,8},{8,12},{12,16},{16,20},{20,24},{24,28},{28,32},{32,36}... | collective-permute-start | bytes 786440 | tf_op jit(solution)/shard_map/ppermute | solution.py:21
  181.5 7.1 %collective-permute-start.9 = (f32[1,32,4,512]{3,2,1,0:T(4,128)S(1)}, f32[1,32,4,512]{3,2,1,0:T(4,128)S(1)}, u32[]{:S(2)}, u32[]{:S(2)}) collective-permute-start(f32[1,32,4,512]{3,2,1,0:T(4,128)S(1)} %get-tuple-element.14), channel_id=1, source_target_pairs={{4,0},{8,4},{12,8},{16,12},{20,16},{24,20},{28,24},{32,28},{36,32}... | collective-permute-start | bytes 786440 | tf_op jit(solution)/shard_map/ppermute | solution.py:23
  202.4 13.4 %copy-start.3 = (s32[1,32,16,512]{3,2,1,0:T(8,128)S(1)}, s32[1,32,16,512]{3,2,1,0:T(8,128)}, u32[]{:S(2)}) copy-start(s32[1,32,16,512]{3,2,1,0:T(8,128)} %param.3) | copy-start | bytes 3145732
  203.8 8.1 %collective-permute-start.11 = (f32[1,32,4,512]{3,2,1,0:T(4,128)S(1)}, f32[1,32,4,512]{3,2,1,0:T(4,128)S(1)}, u32[]{:S(2)}, u32[]{:S(2)}) collective-permute-start(f32[1,32,4,512]{3,2,1,0:T(4,128)S(1)} %get-tuple-element.11), channel_id=1, source_target_pairs={{4,0},{8,4},{12,8},{16,12},{20,16},{24,20},{28,24},{32,28},{36,32}... | collective-permute-start | bytes 786440 | tf_op jit(solution)/shard_map/ppermute | solution.py:23
  205.1 8.2 %collective-permute-start.10 = (f32[1,32,4,512]{3,2,1,0:T(4,128)S(1)}, f32[1,32,4,512]{3,2,1,0:T(4,128)S(1)}, u32[]{:S(2)}, u32[]{:S(2)}) collective-permute-start(f32[1,32,4,512]{3,2,1,0:T(4,128)S(1)} %get-tuple-element.12), channel_id=1, source_target_pairs={{0,4},{4,8},{8,12},{12,16},{16,20},{20,24},{24,28},{28,32},{32,36}... | collective-permute-start | bytes 786440 | tf_op jit(solution)/shard_map/ppermute | solution.py:21
  211.9 1.5 copy-start.5
  213.3 2.4 copy-start.6
Sparse Core Ops, SparseCore 0:
  9.1 70.6 all-gather.1
  229.1 67.2 reduce-scatter.1
where the time goes:
time: 383 us; the launch traced here: 382 us
  waiting for transfers between devices  173 us (45%)
  other arithmetic  76.4 us (20%)
  blocking collectives  75.1 us (20%)
  starting transfers between devices  37.6 us (10%)
  between operations  14.3 us (4%)
  local copies, waits for them, and re-layouts  5.69 us (1%)
    psum x1, blocking collectives, body(): squares = lax.psum(jnp.sum(share * share), ('slab', 'probe'))  75.1 us
    all_gather x1, waiting for transfers between devices, body(): gathered = lax.all_gather(snapshots, 'probe', axis=0, tiled=True)  72.6 us
    reduce_scatter x1, waiting for transfers between devices, body(): share = lax.psum_scatter(estimate, 'probe', scatter_dimension=2, tiled=True)  67.4 us
    mul x3, other arithmetic, body(): coeff_field * adjoint  33.9 us
    ppermute x6, starting transfers between devices, extended_2(): lax.ppermute(tail, axis, [(i, (i + 1) % count) for i in range(ends)])  29.3 us
    ppermute x6, waiting for transfers between devices, extended_2(): lax.ppermute(head, axis, [((i + 1) % count, i) for i in range(ends)])  23.4 us
    reduce_sum x1, other arithmetic, body(): estimate = jnp.sum(signs * image, axis=0)  13.2 us
    add x2, other arithmetic, body(): 2.0 * current - previous + coeff_field * laplace(current)  12.9 us
  transfers between devices with their start and end apart: 14, of which 14 were waited for; matrix products, arithmetic and copies ran while one was open for 0% of the time, Pallas kernels for 0%

commit v1 on v0

v1 whole, which is shorter than its diff:
```python
import functools

import jax
import jax.numpy as jnp
from jax import lax
from jax.experimental import pallas as pl
from jax.experimental.pallas import tpu as pltpu
from jax.sharding import PartitionSpec as P

NT = 4
COEFFS = (-205.0 / 72.0, 8.0 / 5.0, -1.0 / 5.0, 8.0 / 315.0, -1.0 / 560.0)
EPSILON = 1e-06
AXES = ("slab", "probe")
ROW = (16, 8, 128)
HALF = (4,) + ROW
VLIM = 12 * 1024 * 1024


def call(body, outs, n_smem, n_vmem, flops=1 << 20, nbytes=1 << 20, name=None):
    return pl.pallas_call(
        body,
        out_shape=[jax.ShapeDtypeStruct(s, jnp.float32) for s in outs],
        in_specs=[pl.BlockSpec(memory_space=pltpu.SMEM)] * n_smem
        + [pl.BlockSpec(memory_space=pltpu.VMEM)] * n_vmem,
        out_specs=[pl.BlockSpec(memory_space=pltpu.VMEM) for _ in outs],
        compiler_params=pltpu.CompilerParams(vmem_limit_bytes=VLIM),
        cost_estimate=pl.CostEstimate(flops=flops, bytes_accessed=nbytes, transcendentals=0),
        name=name,
    )


def place(y):
    owner = y // 8
    j = y if owner == 0 else 15 - y
    half = j // 4
    return owner, half, (j if half == 0 else 7 - j)


def pick(rows_ref, y, zl, zh):
    start = ((zh * 16 + zl) * 2 + y // 8) * 32 + y % 8
    return rows_ref[pl.ds(start, 4, stride=8), :]


def pack_u(flags, rows_ref, out_ref):
    core = flags[0]

    def step(zl, carry):
        for y in range(16):
            owner, half, k = place(y)
            slot = jnp.where(core == owner, 0, 1)
            for zh in range(2):
                out_ref[slot, half, k, zl, zh * 4 : zh * 4 + 4, :] = pick(rows_ref, y, zl, zh)
        return carry

    lax.fori_loop(0, 16, step, 0)


def pack_sk(flags, probe_ref, kappa_ref, sign_ref, k_ref):
    core = flags[0]

    def step(zl, carry):
        for y in range(16):
            owner, half, k = place(y)
            slot = jnp.where(core == owner, 0, 1)
            for zh in range(2):
                bits = pick(probe_ref, y, zl, zh)
                sign_ref[slot, half, k, zl, zh * 4 : zh * 4 + 4, :] = (2 * bits - 1).astype(jnp.float32)
                k_ref[slot, half, k, zl, zh * 4 : zh * 4 + 4, :] = pick(kappa_ref, y, zl, zh)
        return carry

    lax.fori_loop(0, 16, step, 0)


def sort_u(flags, own_ref, got_ref, even_ref, oddo_ref, oddi_ref):
    first = flags[0] == 0

    def step(k, carry):
        for half in range(2):
            own, got = own_ref[0, half, k], got_ref[half, k]
            even_ref[half, k] = jnp.where(first, own, got)
            (oddo_ref if half == 0 else oddi_ref)[k] = jnp.where(first, got, own)
        return carry

    lax.fori_loop(0, 4, step, 0)


def sort_s(flags, own_ref, got_ref, so_ref, si_ref):
    first = flags[0] == 0

    def step(k, carry):
        for half in range(2):
            own, got = own_ref[0, half, k], got_ref[half, k]
            out = so_ref if half == 0 else si_ref
            out[0, k] = jnp.where(first, own, got)
            out[1, k] = jnp.where(first, got, own)
        return carry

    lax.fori_loop(0, 4, step, 0)


def start_fields(flags, le_ref, re_ref, so_ref, si_ref, fo_ref, fi_ref):
    low = flags[1] == 0

    def step(k, carry):
        for half in range(2):
            u = jnp.where(low, le_ref[half, k], re_ref[half, k])
            s_ref, f_ref = (so_ref, fo_ref) if half == 0 else (si_ref, fi_ref)
            for p in range(2):
                f_ref[p, k] = s_ref[p, k] * u
        return carry

    lax.fori_loop(0, 4, step, 0)


def laplace_row(rows, k):
    centre = rows[k + 4]
    sub = lax.broadcasted_iota(jnp.int32, (1, 8, 128), 1)
    lane = lax.broadcasted_iota(jnp.int32, (1, 8, 128), 2)
    upper = sub >= 4
    tile = sub % 4
    zero = jnp.zeros((1, 8, 128), jnp.float32)
    above = jnp.where(upper, pltpu.roll(centre[12:16], 4, 1), zero)
    below = jnp.where(upper, zero, pltpu.roll(centre[0:4], 4, 1))
    column = jnp.concatenate([above, centre, below], axis=0)
    following = jnp.where(tile == 3, zero, pltpu.roll(centre, 7, 1))
    preceding = jnp.where(tile == 0, zero, pltpu.roll(centre, 1, 1))
    edge = jnp.where(lane < 64, following, preceding)
    total = (3.0 * COEFFS[0]) * centre
    for j in range(1, 5):
        paired = column[4 + j : 20 + j] + column[4 - j : 20 - j]
        paired = paired + (rows[k + 4 + j] + rows[k + 4 - j])
        paired = paired + pltpu.roll(jnp.where(lane >= j, centre, edge), 128 - j, 2)
        paired = paired + pltpu.roll(jnp.where(lane < 128 - j, centre, edge), j, 2)
        total = total + COEFFS[j] * paired
    return total


def rows_of(open_, halo_ref, near_ref, far_ref, p):
    halo = [jnp.where(open_, halo_ref[p, 3 - i], 0.0) for i in range(4)]
    return halo + [near_ref[p, i] for i in range(4)] + [far_ref[p, 3 - i] for i in range(4)]


def forward(outer, first, last, flags, *refs):
    refs = list(refs)
    halo_ref, near_ref, far_ref, s_ref, k_ref, lu_ref, ru_ref = refs[:7]
    old_ref = None if first else refs[7]
    outs = refs[7:] if first else refs[8:]
    low = flags[1] == 0 if not last[1] else flags[1] != 0
    open_ = flags[2] == 0 if outer else True

    def step(p, carry):
        rows = rows_of(open_, halo_ref, near_ref, far_ref, p)
        for k in range(4):
            u = jnp.where(low, lu_ref[k], ru_ref[k])
            value = 2.0 * rows[k + 4] + k_ref[k] * laplace_row(rows, k) + s_ref[p, k] * u
            if not first:
                value = value - old_ref[p, k]
            outs[0][p, k] = value
            if last[0]:
                outs[1][p, k] = k_ref[k] * value
        return carry

    lax.fori_loop(0, 2, step, 0)


def backward(outer, first, flags, *refs):
    refs = list(refs)
    halo_ref, near_ref, far_ref, f_ref, a_ref, k_ref = refs[:6]
    later_ref = None if first else refs[6]
    a_out, g_out = refs[-2:]
    open_ = flags[2] == 0 if outer else True

    def step(p, carry):
        rows = rows_of(open_, halo_ref, near_ref, far_ref, p)
        for k in range(4):
            value = f_ref[p, k] + 2.0 * a_ref[p, k] + laplace_row(rows, k)
            if not first:
                value = value - later_ref[p, k]
            a_out[p, k] = value
            g_out[p, k] = k_ref[k] * value
        return carry

    lax.fori_loop(0, 2, step, 0)


def finish(outer, flags, *refs):
    (halo_ref, near_ref, far_ref, f1_ref, f4_ref, a3_ref, a2_ref, s_ref) = refs[:8]
    le_ref, re_ref, lo_ref, ro_ref, est_ref = refs[8:]
    low = flags[1] == 0
    open_ = flags[2] == 0 if outer else True

    def step(p, carry):
        rows = rows_of(open_, halo_ref, near_ref, far_ref, p)
        for k in range(4):
            a1 = f1_ref[p, k] + 2.0 * a2_ref[p, k] - a3_ref[p, k] + laplace_row(rows, k)
            u0, u2 = jnp.where(low, le_ref[k], re_ref[k]), jnp.where(low, re_ref[k], le_ref[k])
            u1, u3 = jnp.where(low, lo_ref[k], ro_ref[k]), jnp.where(low, ro_ref[k], lo_ref[k])
            image = u3 * f4_ref[p, k] + u2 * a3_ref[p, k] + u1 * a2_ref[p, k] + u0 * a1
            est_ref[k] = jnp.where(p == 0, 0.0, est_ref[k]) + s_ref[p, k] * image
        return carry

    lax.fori_loop(0, 2, step, 0)


def spread(flags, eo_ref, ei_ref, keep_ref, give_ref):
    low = flags[1] == 0
    for half, ref in ((0, eo_ref), (1, ei_ref)):
        for k in range(4):
            j = k if half == 0 else 7 - k

            def step(zl, carry, ref=ref, k=k, j=j):
                value = ref[k, zl]
                for zh in range(2):
                    row = j * 32 + zh * 16 + zl
                    lo, hi = value[zh * 4 : zh * 4 + 2], value[zh * 4 + 2 : zh * 4 + 4]
                    keep_ref[pl.ds(row, 2, stride=256), :] = jnp.where(low, lo, hi)
                    give_ref[pl.ds(row, 2, stride=256), :] = jnp.where(low, hi, lo)
                return carry

            lax.fori_loop(0, 16, step, 0)


def reduce_body(flags, keep_ref, got_ref, mine_ref, give_ref, sq_ref):
    first = flags[0] == 0
    total = jnp.zeros((8, 128), jnp.float32)
    for i in range(8):
        lo = keep_ref[pl.ds(i * 32, 32), :] + got_ref[pl.ds(i * 32, 32), :]
        hi = keep_ref[pl.ds(256 + i * 32, 32), :] + got_ref[pl.ds(256 + i * 32, 32), :]
        mine_ref[pl.ds(i * 32, 32), :] = jnp.where(first, lo, hi)
        give_ref[pl.ds(i * 32, 32), :] = jnp.where(first, hi, lo)
        total = total + jnp.sum((lo * lo + hi * hi).reshape(4, 8, 128), axis=0)
    part = jnp.sum(jnp.sum(total, axis=0, keepdims=True), axis=1, keepdims=True)
    sq_ref[...] = jnp.broadcast_to(part, sq_ref.shape)


def scale_body(cells, flags, sq_ref, mine_ref, got_ref, out_ref):
    squares = jnp.sum(sq_ref[...], axis=0, keepdims=True)
    factor = lax.rsqrt(squares / cells + EPSILON)
    for core in range(2):

        @pl.when(flags[0] == core)
        def _():
            for j in range(8):
                rows = (j, 15 - j) if core == 0 else (15 - j, j)
                out_ref[pl.ds(rows[0], 32, stride=16), :] = mine_ref[pl.ds(j * 32, 32), :] * factor
                out_ref[pl.ds(rows[1], 32, stride=16), :] = got_ref[pl.ds(j * 32, 32), :] * factor


def rows_view(x):
    return x.reshape(32, 2, 8, 4, 128).transpose(0, 1, 3, 2, 4).reshape(2048, 128)


def body(probes, snapshots, kappa):
    n_slab, n_probe = lax.axis_size("slab"), lax.axis_size("probe")
    n = n_slab * n_probe
    slab, probe = lax.axis_index("slab"), lax.axis_index("probe")
    core, chip = probe % 2, probe // 2
    ends = ((core == 0) & (slab == 0)) | ((core == 1) & (slab == n_slab - 1))
    flags = jnp.stack([core, chip, ends.astype(jnp.int32)]).astype(jnp.int32)

    def across(x):
        return lax.ppermute(x, AXES, [(i, i ^ 1) for i in range(n)])

    def over(x):
        return lax.ppermute(x, AXES, [(i, i ^ 2) for i in range(n)])

    pairs = []
    for i in range(n):
        s, p = divmod(i, n_probe)
        hi, c = divmod(p, 2)
        t = s + 1 if c == 1 else s - 1
        if t in (-1, n_slab):
            t, hi = t % n_slab, 1 - hi
        pairs.append((i, t * n_probe + hi * 2 + 1 - c))

    def along(x):
        return lax.ppermute(x, AXES, pairs)

    both = (2,) + HALF
    packed = (2, 2) + HALF
    (u_pack,) = call(pack_u, [packed], 1, 1, name="pack_u")(flags, rows_view(snapshots))
    u_got = across(u_pack[1])
    s_pack, k_pack = call(pack_sk, [packed, packed], 1, 2, name="pack_sk")(
        flags, rows_view(probes), rows_view(kappa)
    )
    s_got = across(s_pack[1])
    even, odd_o, odd_i = call(sort_u, [both, HALF, HALF], 1, 2, name="sort_u")(flags, u_pack, u_got)
    r_even = over(even)
    r_odd_o = over(odd_o)
    r_odd_i = over(odd_i)
    signs = call(sort_s, [both, both], 1, 2, name="sort_s")(flags, s_pack, s_got)
    kap = (k_pack[0, 0], k_pack[0, 1])
    ev, rev = (even[0], even[1]), (r_even[0], r_even[1])
    odd, rodd = (odd_o, odd_i), (r_odd_o, r_odd_i)

    f1 = call(start_fields, [both, both], 1, 4, name="start")(flags, even, r_even, *signs)

    def halos(f):
        return along(f[0]), across(f[1])

    def halves(make):
        inner = make(1)
        outer = make(0)
        return outer, inner

    def fwd(f, old, u, ru, last, name):
        halo = halos(f)

        def make(h):
            ins = [halo[h], f[h], f[1 - h], signs[h], kap[h], u[h], ru[h]]
            if old is not None:
                ins.append(old[h])
            outs = [both] * (2 if last[0] else 1)
            kern = functools.partial(forward, h == 0, old is None, last)
            return call(kern, outs, 1, len(ins), name=name + "oi"[h])(flags, *ins)

        outer, inner = halves(make)
        return [(outer[i], inner[i]) for i in range(len(outer))]

    (f2,) = fwd(f1, None, odd, rodd, (False, False), "f2")
    (f3,) = fwd(f2, f1, ev, rev, (False, True), "f3")
    f4, g4 = fwd(f3, f2, odd, rodd, (True, True), "f4")

    def bwd(g, f, a, later, name):
        halo = halos(g)

        def make(h):
            ins = [halo[h], g[h], g[1 - h], f[h], a[h], kap[h]]
            if later is not None:
                ins.append(later[h])
            kern = functools.partial(backward, h == 0, later is None)
            return call(kern, [both, both], 1, len(ins), name=name + "oi"[h])(flags, *ins)

        outer, inner = halves(make)
        return [(outer[i], inner[i]) for i in range(2)]

    a3, g3 = bwd(g4, f3, f4, None, "a3")
    a2, g2 = bwd(g3, f2, a3, f4, "a2")
    halo = halos(g2)

    def last(h):
        ins = [halo[h], g2[h], g2[1 - h], f1[h], f4[h], a3[h], a2[h], signs[h]]
        ins += [ev[h], rev[h], odd[h], rodd[h]]
        kern = functools.partial(finish, h == 0)
        return call(kern, [HALF], 1, len(ins), name="a1" + "oi"[h])(flags, *ins)[0]

    est_i = last(1)
    est_o = last(0)
    keep, give = call(spread, [(512, 128), (512, 128)], 1, 2, name="spread")(flags, est_o, est_i)
    got = over(give)
    mine, send, squares = call(
        reduce_body, [(256, 128), (256, 128), (n, 128)], 1, 2, name="reduce"
    )(flags, keep, got)
    theirs = across(send)
    squares = lax.all_to_all(squares, AXES, 0, 0, tiled=True)
    cells = 32.0 * 16.0 * 512.0 * n_slab
    (out,) = call(functools.partial(scale_body, cells), [(512, 128)], 1, 3, name="scale")(
        flags, squares, mine, theirs
    )
    return out.reshape(32, 16, 128)


def solution(mesh):
    return jax.shard_map(
        body,
        mesh=mesh,
        in_specs=(
            P("probe", None, "slab", None),
            P("probe", None, "slab", None),
            P(None, "slab", None),
        ),
        out_specs=P(None, "slab", "probe"),
        check_vma=False,
    )
```

time: 383 us -> 190 us (0.50)
  waiting for transfers between devices: 173 us -> 46.6 us
  other arithmetic: 76.4 us -> 0.08 us
  blocking collectives: 75.1 us -> 0 us
  starting transfers between devices: 37.6 us -> 108 us
  Pallas kernels: 0 us -> 33.9 us
  between operations: 14.3 us -> 0.3 us
  local copies, waits for them, and re-layouts: 5.69 us -> 1.41 us
    psum x1 -> x0, blocking collectives: 75.1 us -> none  [body(): squares = lax.psum(jnp.sum(share * share), ('slab', 'probe'))]
    all_gather x1 -> x0, waiting for transfers between devices: 72.6 us -> none  [body(): gathered = lax.all_gather(snapshots, 'probe', axis=0, tiled=True)]
    reduce_scatter x1 -> x0, waiting for transfers between devices: 67.4 us -> none  [body(): share = lax.psum_scatter(estimate, 'probe', scatter_dimension=2, tiled=True)]
    ppermute x12 -> x19, starting transfers between devices: 37.5 us -> 91.9 us  [the longest x9 78.6 us: across(): return lax.ppermute(x, AXES, [(i, i ^ 1) for i in range(n)])]
    mul x4 -> x0, other arithmetic: 35.7 us -> none  [the longest x3 33.9 us: body(): coeff_field * adjoint]
    pallas_call x0 -> x20, Pallas kernels: none -> 33.9 us  [the longest x6 12.8 us: make(): return call(kern, outs, 1, len(ins), name=name + 'oi'[h])(flags, *ins)]
    all_to_all x0 -> x1, starting transfers between devices: none -> 15.7 us  [body(): squares = lax.all_to_all(squares, AXES, 0, 0, tiled=True)]
    reduce_sum x2 -> x0, other arithmetic: 14.8 us -> none  [the longest x1 13.2 us: body(): estimate = jnp.sum(signs * image, axis=0)]
  transfers between devices with their start and end apart: 14 -> 20, of which waited for: 14 -> 6; matrix products, arithmetic and copies ran while one was open for 0% -> 0% of each run, Pallas kernels for 0% -> 14%
where the time goes in v1:
time: 190 us
  starting transfers between devices  108 us (57%)
  waiting for transfers between devices  46.6 us (25%)
  Pallas kernels  33.9 us (18%)
    ppermute x9, starting transfers between devices, across(): return lax.ppermute(x, AXES, [(i, i ^ 1) for i in range(n)])  78.6 us
    ppermute x4, waiting for transfers between devices, over(): return lax.ppermute(x, AXES, [(i, i ^ 2) for i in range(n)])  36 us
    all_to_all x1, starting transfers between devices, body(): squares = lax.all_to_all(squares, AXES, 0, 0, tiled=True)  15.7 us
    pallas_call x6, Pallas kernels, make(): return call(kern, outs, 1, len(ins), name=name + 'oi'[h])(flags, *ins)  12.8 us
    ppermute x4, starting transfers between devices, over(): return lax.ppermute(x, AXES, [(i, i ^ 2) for i in range(n)])  10.8 us
    all_to_all x1, waiting for transfers between devices, body(): squares = lax.all_to_all(squares, AXES, 0, 0, tiled=True)  9.64 us
    pallas_call x4, Pallas kernels, make(): call(kern, [both, both], 1, len(ins), name=name + 'oi'[h])(flags, *ins)  8.23 us
    pallas_call x2, Pallas kernels, last(): return call(kern, [HALF], 1, len(ins), name='a1' + 'oi'[h])(flags, *ins)[0]  4.76 us
  transfers between devices with their start and end apart: 20, of which 6 were waited for; matrix products, arithmetic and copies ran while one was open for 0% of the time, Pallas kernels for 14%

profile of v1, /device:TPU:1, one launch (start us, length us, event | category | flops | bytes accessed | tf_op | source)
XLA Modules:
  0.0 189.9 jit_solution(5147362322380106697)
XLA Ops:
  0.0 0.1 pad_add_fusion.flags
  0.1 1.2 copy-done
  1.3 0.8 pack_u.1.own_ref
  2.2 0.0 copy-start.1
  2.2 3.3 %collective-permute-start = (f32[2,4,16,8,128]{4,3,2,1,0:T(8,128)S(1)}, f32[2,4,16,8,128]{4,3,2,1,0:T(8,128)S(1)}, u32[]{:S(2)}, u32[]{:S(2)}) collective-permute-start(f32[2,4,16,8,128]{4,3,2,1,0:T(8,128)S(1)} %slice_bitcast_fusion), channel_id=1, source_target_pairs={{0,1},{1,0},{2,3},{3,2},{4,5},{5,4},{6,7},{7,6},{8,9},{9,8},{10,11... | collective-permute-start | bytes 1572872 | tf_op jit(solution)/shard_map/ppermute | solution.py:262
  5.5 0.0 copy-done.2
  5.5 1.2 pack_sk.1
  6.8 1.2 collective-permute-start.2
  8.0 0.0 collective-permute-done.got_ref
  8.0 0.6 sort_u.1
  8.7 5.3 %collective-permute-start.1 = (f32[2,4,16,8,128]{4,3,2,1,0:T(8,128)S(1)}, f32[2,4,16,8,128]{4,3,2,1,0:T(8,128)S(1)}, u32[]{:S(2)}, u32[]{:S(2)}) collective-permute-start(f32[2,4,16,8,128]{4,3,2,1,0:T(8,128)S(1)} %get-tuple-element.31.le_ref), channel_id=1, source_target_pairs={{0,2},{1,3},{2,0},{3,1},{4,6},{5,7},{6,4},{7,5},{8,10},{9,11},{10,... | collective-permute-start | bytes 1572872 | tf_op jit(solution)/shard_map/ppermute | solution.py:265
  14.0 0.0 collective-permute-done.2.got_ref
  14.0 0.6 sort_s.1
  14.6 13.7 %collective-permute-done.1.re_ref = f32[2,4,16,8,128]{4,3,2,1,0:T(8,128)S(1)} collective-permute-done((f32[2,4,16,8,128]{4,3,2,1,0:T(8,128)S(1)}, f32[2,4,16,8,128]{4,3,2,1,0:T(8,128)S(1)}, u32[]{:S(2)}, u32[]{:S(2)}) %collective-permute-start.1) | collective-permute-done | bytes 524320 | tf_op jit(solution)/shard_map/ppermute | solution.py:265
  28.3 0.7 start.1
  28.9 2.1 %collective-permute-start.3 = (f32[2,4,16,8,128]{4,3,2,1,0:T(8,128)S(1)}, f32[2,4,16,8,128]{4,3,2,1,0:T(8,128)S(1)}, u32[]{:S(2)}, u32[]{:S(2)}) collective-permute-start(f32[2,4,16,8,128]{4,3,2,1,0:T(8,128)S(1)} %get-tuple-element.35.refs_1_.refs_2_.refs_7_.refs_3_), channel_id=1, source_target_pairs={{0,255},{1,4},{2,253},{3,6},{4,1},{5,8},{6,3},{7,10},{8,5},{9,12},... | collective-permute-start | bytes 1572872 | tf_op jit(solution)/shard_map/ppermute | solution.py:277
  31.0 12.3 %collective-permute-start.6 = (f32[2,4,16,8,128]{4,3,2,1,0:T(8,128)S(1)}, f32[2,4,16,8,128]{4,3,2,1,0:T(8,128)S(1)}, u32[]{:S(2)}, u32[]{:S(2)}) collective-permute-start(f32[2,4,16,8,128]{4,3,2,1,0:T(8,128)S(1)} %get-tuple-element.36.refs_2_.refs_1_.refs_7_.refs_3_), channel_id=1, source_target_pairs={{0,1},{1,0},{2,3},{3,2},{4,5},{5,4},{6,7},{7,6},{8,9},{9,8},{10,11... | collective-permute-start | bytes 1572872 | tf_op jit(solution)/shard_map/ppermute | solution.py:262
  43.3 1.5 collective-permute-start.4
  44.8 3.9 %collective-permute-start.7 = (f32[4,16,8,128]{3,2,1,0:T(8,128)S(1)}, f32[4,16,8,128]{3,2,1,0:T(8,128)S(1)}, u32[]{:S(2)}, u32[]{:S(2)}) collective-permute-start(f32[4,16,8,128]{3,2,1,0:T(8,128)S(1)} %get-tuple-element.39.refs_5_.refs_10_), channel_id=1, source_target_pairs={{0,2},{1,3},{2,0},{3,1},{4,6},{5,7},{6,4},{7,5},{8,10},{9,11},{10,... | collective-permute-start | bytes 786440 | tf_op jit(solution)/shard_map/ppermute | solution.py:265
  48.7 6.7 %collective-permute-done.4.refs_6_.refs_11_ = f32[4,16,8,128]{3,2,1,0:T(8,128)S(1)} collective-permute-done((f32[4,16,8,128]{3,2,1,0:T(8,128)S(1)}, f32[4,16,8,128]{3,2,1,0:T(8,128)S(1)}, u32[]{:S(2)}, u32[]{:S(2)}) %collective-permute-start.4) | collective-permute-done | bytes 262176 | tf_op jit(solution)/shard_map/ppermute | solution.py:265
  55.4 0.0 collective-permute-done.3.refs_0_
  55.4 2.1 %f2o.1.refs_1_.refs_2_.refs_7_.refs_3_ = f32[2,4,16,8,128]{4,3,2,1,0:T(8,128)S(1)} custom-call(s32[3]{0:T(128)S(1)} %pad_add_fusion.flags, f32[2,4,16,8,128]{4,3,2,1,0:T(8,128)S(1)} %collective-permute-done.3.refs_0_, f32[2,4,16,8,128]{4,3,2,1,0:T(8,128)S(1)} %get-tuple-element.35.refs_1_.refs_2_.refs_7_.refs_3_, ...), custom_call_target="tpu_custom_call" | custom-call | flops 1048576 | bytes 1048576 | tf_op jit(solution)/shard_map/f2o/pallas_call | solution.py:315
  57.5 0.1 collective-permute-start.5
  57.6 3.7 %collective-permute-done.7.refs_6_.refs_11_ = f32[4,16,8,128]{3,2,1,0:T(8,128)S(1)} collective-permute-done((f32[4,16,8,128]{3,2,1,0:T(8,128)S(1)}, f32[4,16,8,128]{3,2,1,0:T(8,128)S(1)}, u32[]{:S(2)}, u32[]{:S(2)}) %collective-permute-start.7) | collective-permute-done | bytes 262176 | tf_op jit(solution)/shard_map/ppermute | solution.py:265
  61.3 0.0 collective-permute-done.6.refs_0_
  61.3 2.1 %f2i.1.refs_2_.refs_1_.refs_7_.refs_3_ = f32[2,4,16,8,128]{4,3,2,1,0:T(8,128)S(1)} custom-call(s32[3]{0:T(128)S(1)} %pad_add_fusion.flags, f32[2,4,16,8,128]{4,3,2,1,0:T(8,128)S(1)} %collective-permute-done.6.refs_0_, f32[2,4,16,8,128]{4,3,2,1,0:T(8,128)S(1)} %get-tuple-element.36.refs_2_.refs_1_.refs_7_.refs_3_, ...), custom_call_target="tpu_custom_call" | custom-call | flops 1048576 | bytes 1048576 | tf_op jit(solution)/shard_map/f2i/pallas_call | solution.py:315
  63.4 11.0 %collective-permute-start.9 = (f32[2,4,16,8,128]{4,3,2,1,0:T(8,128)S(1)}, f32[2,4,16,8,128]{4,3,2,1,0:T(8,128)S(1)}, u32[]{:S(2)}, u32[]{:S(2)}) collective-permute-start(f32[2,4,16,8,128]{4,3,2,1,0:T(8,128)S(1)} %f2i.1.refs_2_.refs_1_.refs_7_.refs_3_), channel_id=1, source_target_pairs={{0,1},{1,0},{2,3},{3,2},{4,5},{5,4},{6,7},{7,6},{8,9},{9,8},{10,11... | collective-permute-start | bytes 1572872 | tf_op jit(solution)/shard_map/ppermute | solution.py:262
  74.5 0.0 collective-permute-done.5.refs_0_
  74.5 2.1 %f3o.1.refs_1_.refs_2_.refs_3_ = f32[2,4,16,8,128]{4,3,2,1,0:T(8,128)S(1)} custom-call(s32[3]{0:T(128)S(1)} %pad_add_fusion.flags, f32[2,4,16,8,128]{4,3,2,1,0:T(8,128)S(1)} %collective-permute-done.5.refs_0_, f32[2,4,16,8,128]{4,3,2,1,0:T(8,128)S(1)} %f2o.1.refs_1_.refs_2_.refs_7_.refs_3_, f32[2,4,16,8,128]{4,3,2,1,0:T(8,128)S(1)} %f2i.1.refs_2_.refs_1_.refs_7_.refs_3_, ...), custom_call_target="tpu_custom_call" | custom-call | flops 1048576 | bytes 1048576 | tf_op jit(solution)/shard_map/f3o/pallas_call | solution.py:315
  76.7 0.1 collective-permute-start.8
  76.8 0.0 collective-permute-done.9.refs_0_
  76.8 2.1 %f3i.1.refs_2_.refs_1_.refs_3_ = f32[2,4,16,8,128]{4,3,2,1,0:T(8,128)S(1)} custom-call(s32[3]{0:T(128)S(1)} %pad_add_fusion.flags, f32[2,4,16,8,128]{4,3,2,1,0:T(8,128)S(1)} %collective-permute-done.9.refs_0_, f32[2,4,16,8,128]{4,3,2,1,0:T(8,128)S(1)} %f2i.1.refs_2_.refs_1_.refs_7_.refs_3_, f32[2,4,16,8,128]{4,3,2,1,0:T(8,128)S(1)} %f2o.1.refs_1_.refs_2_.refs_7_.refs_3_, ...), custom_call_target="tpu_custom_call" | custom-call | flops 1048576 | bytes 1048576 | tf_op jit(solution)/shard_map/f3i/pallas_call | solution.py:315
  78.9 13.0 %collective-permute-start.11 = (f32[2,4,16,8,128]{4,3,2,1,0:T(8,128)S(1)}, f32[2,4,16,8,128]{4,3,2,1,0:T(8,128)S(1)}, u32[]{:S(2)}, u32[]{:S(2)}) collective-permute-start(f32[2,4,16,8,128]{4,3,2,1,0:T(8,128)S(1)} %f3i.1.refs_2_.refs_1_.refs_3_), channel_id=1, source_target_pairs={{0,1},{1,0},{2,3},{3,2},{4,5},{5,4},{6,7},{7,6},{8,9},{9,8},{10,11... | collective-permute-start | bytes 1572872 | tf_op jit(solution)/shard_map/ppermute | solution.py:262
  91.9 0.0 collective-permute-done.8.refs_0_
  91.9 2.1 %f4o.1 = (f32[2,4,16,8,128]{4,3,2,1,0:T(8,128)S(1)}, f32[2,4,16,8,128]{4,3,2,1,0:T(8,128)S(1)}) custom-call(s32[3]{0:T(128)S(1)} %pad_add_fusion.flags, f32[2,4,16,8,128]{4,3,2,1,0:T(8,128)S(1)} %collective-permute-done.8.refs_0_, f32[2,4,16,8,128]{4,3,2,1,0:T(8,128)S(1)} %f3o.1.refs_1_.refs_2_.refs_3_, ...), custom_call_target="tpu_custom_call" | custom-call | flops 1048576 | bytes 1048576 | tf_op jit(solution)/shard_map/f4o/pallas_call | solution.py:315
  94.0 0.1 collective-permute-start.10
  94.1 0.0 collective-permute-done.11.refs_0_
  94.2 2.1 %f4i.1 = (f32[2,4,16,8,128]{4,3,2,1,0:T(8,128)S(1)}, f32[2,4,16,8,128]{4,3,2,1,0:T(8,128)S(1)}) custom-call(s32[3]{0:T(128)S(1)} %pad_add_fusion.flags, f32[2,4,16,8,128]{4,3,2,1,0:T(8,128)S(1)} %collective-permute-done.11.refs_0_, f32[2,4,16,8,128]{4,3,2,1,0:T(8,128)S(1)} %f3i.1.refs_2_.refs_1_.refs_3_, ...), custom_call_target="tpu_custom_call" | custom-call | flops 1048576 | bytes 1048576 | tf_op jit(solution)/shard_map/f4i/pallas_call | solution.py:315
  96.3 12.0 %collective-permute-start.13 = (f32[2,4,16,8,128]{4,3,2,1,0:T(8,128)S(1)}, f32[2,4,16,8,128]{4,3,2,1,0:T(8,128)S(1)}, u32[]{:S(2)}, u32[]{:S(2)}) collective-permute-start(f32[2,4,16,8,128]{4,3,2,1,0:T(8,128)S(1)} %get-tuple-element.41.refs_2_.refs_1_), channel_id=1, source_target_pairs={{0,1},{1,0},{2,3},{3,2},{4,5},{5,4},{6,7},{7,6},{8,9},{9,8},{10,11... | collective-permute-start | bytes 1572872 | tf_op jit(solution)/shard_map/ppermute | solution.py:262
  108.3 0.0 collective-permute-done.10.refs_0_
  108.3 2.1 %a3o.1 = (f32[2,4,16,8,128]{4,3,2,1,0:T(8,128)S(1)}, f32[2,4,16,8,128]{4,3,2,1,0:T(8,128)S(1)}) custom-call(s32[3]{0:T(128)S(1)} %pad_add_fusion.flags, f32[2,4,16,8,128]{4,3,2,1,0:T(8,128)S(1)} %collective-permute-done.10.refs_0_, f32[2,4,16,8,128]{4,3,2,1,0:T(8,128)S(1)} %get-tuple-element.40.refs_1_.refs_2_, ...), custom_call_target="tpu_custom_call" | custom-call | flops 1048576 | bytes 1048576 | tf_op jit(solution)/shard_map/a3o/pallas_call | solution.py:332
  110.4 0.1 collective-permute-start.12
  110.5 0.0 collective-permute-done.13.refs_0_
  110.5 2.1 %a3i.1 = (f32[2,4,16,8,128]{4,3,2,1,0:T(8,128)S(1)}, f32[2,4,16,8,128]{4,3,2,1,0:T(8,128)S(1)}) custom-call(s32[3]{0:T(128)S(1)} %pad_add_fusion.flags, f32[2,4,16,8,128]{4,3,2,1,0:T(8,128)S(1)} %collective-permute-done.13.refs_0_, f32[2,4,16,8,128]{4,3,2,1,0:T(8,128)S(1)} %get-tuple-element.41.refs_2_.refs_1_, ...), custom_call_target="tpu_custom_call" | custom-call | flops 1048576 | bytes 1048576 | tf_op jit(solution)/shard_map/a3i/pallas_call | solution.py:332
  112.5 11.6 %collective-permute-start.15 = (f32[2,4,16,8,128]{4,3,2,1,0:T(8,128)S(1)}, f32[2,4,16,8,128]{4,3,2,1,0:T(8,128)S(1)}, u32[]{:S(2)}, u32[]{:S(2)}) collective-permute-start(f32[2,4,16,8,128]{4,3,2,1,0:T(8,128)S(1)} %get-tuple-element.45.refs_2_.refs_1_), channel_id=1, source_target_pairs={{0,1},{1,0},{2,3},{3,2},{4,5},{5,4},{6,7},{7,6},{8,9},{9,8},{10,11... | collective-permute-start | bytes 1572872 | tf_op jit(solution)/shard_map/ppermute | solution.py:262
  124.2 0.0 collective-permute-done.12.refs_0_
  124.2 2.1 %a2o.1 = (f32[2,4,16,8,128]{4,3,2,1,0:T(8,128)S(1)}, f32[2,4,16,8,128]{4,3,2,1,0:T(8,128)S(1)}) custom-call(s32[3]{0:T(128)S(1)} %pad_add_fusion.flags, f32[2,4,16,8,128]{4,3,2,1,0:T(8,128)S(1)} %collective-permute-done.12.refs_0_, f32[2,4,16,8,128]{4,3,2,1,0:T(8,128)S(1)} %get-tuple-element.43.refs_1_.refs_2_, ...), custom_call_target="tpu_custom_call" | custom-call | flops 1048576 | bytes 1048576 | tf_op jit(solution)/shard_map/a2o/pallas_call | solution.py:332
  126.3 0.1 collective-permute-start.14
  126.4 0.0 collective-permute-done.15.refs_0_
  126.4 2.1 %a2i.1 = (f32[2,4,16,8,128]{4,3,2,1,0:T(8,128)S(1)}, f32[2,4,16,8,128]{4,3,2,1,0:T(8,128)S(1)}) custom-call(s32[3]{0:T(128)S(1)} %pad_add_fusion.flags, f32[2,4,16,8,128]{4,3,2,1,0:T(8,128)S(1)} %collective-permute-done.15.refs_0_, f32[2,4,16,8,128]{4,3,2,1,0:T(8,128)S(1)} %get-tuple-element.45.refs_2_.refs_1_, ...), custom_call_target="tpu_custom_call" | custom-call | flops 1048576 | bytes 1048576 | tf_op jit(solution)/shard_map/a2i/pallas_call | solution.py:332
  128.5 11.9 %collective-permute-start.16 = (f32[2,4,16,8,128]{4,3,2,1,0:T(8,128)S(1)}, f32[2,4,16,8,128]{4,3,2,1,0:T(8,128)S(1)}, u32[]{:S(2)}, u32[]{:S(2)}) collective-permute-start(f32[2,4,16,8,128]{4,3,2,1,0:T(8,128)S(1)} %get-tuple-element.49.refs_2_.refs_1_), channel_id=1, source_target_pairs={{0,1},{1,0},{2,3},{3,2},{4,5},{5,4},{6,7},{7,6},{8,9},{9,8},{10,11... | collective-permute-start | bytes 1572872 | tf_op jit(solution)/shard_map/ppermute | solution.py:262
  140.4 0.0 collective-permute-done.14.refs_0_
  140.4 2.4 %a1o.1.eo_ref = f32[4,16,8,128]{3,2,1,0:T(8,128)S(1)} custom-call(s32[3]{0:T(128)S(1)} %pad_add_fusion.flags, f32[2,4,16,8,128]{4,3,2,1,0:T(8,128)S(1)} %collective-permute-done.14.refs_0_, f32[2,4,16,8,128]{4,3,2,1,0:T(8,128)S(1)} %get-tuple-element.47.refs_1_.refs_2_, f32[2,4,16,8,128]{4,3,2,1,0:T(8,128)S(1)} %get-tuple-element.49.refs_2_.refs_1_, ...), custom_call_target="tpu_custom_call" | custom-call | flops 1048576 | bytes 1048576 | tf_op jit(solution)/shard_map/a1o/pallas_call | solution.py:345
  142.8 0.0 collective-permute-done.16.refs_0_
  142.8 2.4 %a1i.1.ei_ref = f32[4,16,8,128]{3,2,1,0:T(8,128)S(1)} custom-call(s32[3]{0:T(128)S(1)} %pad_add_fusion.flags, f32[2,4,16,8,128]{4,3,2,1,0:T(8,128)S(1)} %collective-permute-done.16.refs_0_, f32[2,4,16,8,128]{4,3,2,1,0:T(8,128)S(1)} %get-tuple-element.49.refs_2_.refs_1_, f32[2,4,16,8,128]{4,3,2,1,0:T(8,128)S(1)} %get-tuple-element.47.refs_1_.refs_2_, ...), custom_call_target="tpu_custom_call" | custom-call | flops 1048576 | bytes 1048576 | tf_op jit(solution)/shard_map/a1i/pallas_call | solution.py:345
  145.2 1.4 spread.1
  146.6 0.1 collective-permute-start.17
  146.7 12.0 %collective-permute-done.17.got_ref = f32[512,128]{1,0:T(8,128)S(1)} collective-permute-done((f32[512,128]{1,0:T(8,128)S(1)}, f32[512,128]{1,0:T(8,128)S(1)}, u32[]{:S(2)}, u32[]{:S(2)}) %collective-permute-start.17) | collective-permute-done | bytes 262176 | tf_op jit(solution)/shard_map/ppermute | solution.py:265
  158.7 1.3 reduce.1
  160.0 15.7 %all-to-all-start = ((f32[256,1,128]{2,1,0:T(1,128)}), f32[256,1,128]{2,1,0:T(1,128)S(1)}, u32[]{:S(2)}, u32[]{:S(2)}) async-start(f32[256,1,128]{2,1,0:T(1,128)} %bitcast.21), calls=%async_computation | async-start | bytes 262144 | tf_op jit(solution)/shard_map/all_to_all | solution.py:355
  175.7 2.2 %collective-permute-start.18 = (f32[256,128]{1,0:T(8,128)S(1)}, f32[256,128]{1,0:T(8,128)S(1)}, u32[]{:S(2)}, u32[]{:S(2)}) collective-permute-start(f32[256,128]{1,0:T(8,128)S(1)} %get-tuple-element.56), channel_id=1, source_target_pairs={{0,1},{1,0},{2,3},{3,2},{4,5},{5,4},{6,7},{7,6},{8,9},{9,8},{10,11... | collective-permute-start | bytes 393224 | tf_op jit(solution)/shard_map/ppermute | solution.py:262
  177.9 1.0 collective-permute-done.18.got_ref
  178.9 9.6 %all-to-all-done = f32[256,1,128]{2,1,0:T(1,128)S(1)} async-done(((f32[256,1,128]{2,1,0:T(1,128)}), f32[256,1,128]{2,1,0:T(1,128)S(1)}, u32[]{:S(2)}, u32[]{:S(2)}) %all-to-all-start) | async-done | bytes 131104 | tf_op jit(solution)/shard_map/all_to_all | solution.py:355
  188.5 1.4 scale.1
  (8 shorter events, 0.2 us)
Async XLA Ops:
  0.1 1.2 copy-start
  1.3 4.2 %copy-start.2 = (f32[32,16,512]{2,1,0:T(8,128)S(1)}, f32[32,16,512]{2,1,0:T(8,128)}, u32[]{:S(2)}) copy-start(f32[32,16,512]{2,1,0:T(8,128)} %param.5) | copy-start | bytes 3145732
  2.2 3.3 %copy-start.1 = (s32[1,32,16,512]{3,2,1,0:T(8,128)S(1)}, s32[1,32,16,512]{3,2,1,0:T(8,128)}, u32[]{:S(2)}) copy-start(s32[1,32,16,512]{3,2,1,0:T(8,128)} %param.3) | copy-start | bytes 3145732
  2.2 5.8 %collective-permute-start = (f32[2,4,16,8,128]{4,3,2,1,0:T(8,128)S(1)}, f32[2,4,16,8,128]{4,3,2,1,0:T(8,128)S(1)}, u32[]{:S(2)}, u32[]{:S(2)}) collective-permute-start(f32[2,4,16,8,128]{4,3,2,1,0:T(8,128)S(1)} %slice_bitcast_fusion), channel_id=1, source_target_pairs={{0,1},{1,0},{2,3},{3,2},{4,5},{5,4},{6,7},{7,6},{8,9},{9,8},{10,11... | collective-permute-start | bytes 1572872 | tf_op jit(solution)/shard_map/ppermute | solution.py:262
  6.8 7.2 %collective-permute-start.2 = (f32[2,4,16,8,128]{4,3,2,1,0:T(8,128)S(1)}, f32[2,4,16,8,128]{4,3,2,1,0:T(8,128)S(1)}, u32[]{:S(2)}, u32[]{:S(2)}) collective-permute-start(f32[2,4,16,8,128]{4,3,2,1,0:T(8,128)S(1)} %slice_bitcast_fusion.1), channel_id=1, source_target_pairs={{0,1},{1,0},{2,3},{3,2},{4,5},{5,4},{6,7},{7,6},{8,9},{9,8},{10,11... | collective-permute-start | bytes 1572872 | tf_op jit(solution)/shard_map/ppermute | solution.py:262
  8.7 19.6 %collective-permute-start.1 = (f32[2,4,16,8,128]{4,3,2,1,0:T(8,128)S(1)}, f32[2,4,16,8,128]{4,3,2,1,0:T(8,128)S(1)}, u32[]{:S(2)}, u32[]{:S(2)}) collective-permute-start(f32[2,4,16,8,128]{4,3,2,1,0:T(8,128)S(1)} %get-tuple-element.31.le_ref), channel_id=1, source_target_pairs={{0,2},{1,3},{2,0},{3,1},{4,6},{5,7},{6,4},{7,5},{8,10},{9,11},{10,... | collective-permute-start | bytes 1572872 | tf_op jit(solution)/shard_map/ppermute | solution.py:265
  28.9 26.5 %collective-permute-start.3 = (f32[2,4,16,8,128]{4,3,2,1,0:T(8,128)S(1)}, f32[2,4,16,8,128]{4,3,2,1,0:T(8,128)S(1)}, u32[]{:S(2)}, u32[]{:S(2)}) collective-permute-start(f32[2,4,16,8,128]{4,3,2,1,0:T(8,128)S(1)} %get-tuple-element.35.refs_1_.refs_2_.refs_7_.refs_3_), channel_id=1, source_target_pairs={{0,255},{1,4},{2,253},{3,6},{4,1},{5,8},{6,3},{7,10},{8,5},{9,12},... | collective-permute-start | bytes 1572872 | tf_op jit(solution)/shard_map/ppermute | solution.py:277
  31.0 30.3 %collective-permute-start.6 = (f32[2,4,16,8,128]{4,3,2,1,0:T(8,128)S(1)}, f32[2,4,16,8,128]{4,3,2,1,0:T(8,128)S(1)}, u32[]{:S(2)}, u32[]{:S(2)}) collective-permute-start(f32[2,4,16,8,128]{4,3,2,1,0:T(8,128)S(1)} %get-tuple-element.36.refs_2_.refs_1_.refs_7_.refs_3_), channel_id=1, source_target_pairs={{0,1},{1,0},{2,3},{3,2},{4,5},{5,4},{6,7},{7,6},{8,9},{9,8},{10,11... | collective-permute-start | bytes 1572872 | tf_op jit(solution)/shard_map/ppermute | solution.py:262
  43.3 12.1 %collective-permute-start.4 = (f32[4,16,8,128]{3,2,1,0:T(8,128)S(1)}, f32[4,16,8,128]{3,2,1,0:T(8,128)S(1)}, u32[]{:S(2)}, u32[]{:S(2)}) collective-permute-start(f32[4,16,8,128]{3,2,1,0:T(8,128)S(1)} %get-tuple-element.38.refs_5_.refs_10_), channel_id=1, source_target_pairs={{0,2},{1,3},{2,0},{3,1},{4,6},{5,7},{6,4},{7,5},{8,10},{9,11},{10,... | collective-permute-start | bytes 786440 | tf_op jit(solution)/shard_map/ppermute | solution.py:265
  44.8 16.5 %collective-permute-start.7 = (f32[4,16,8,128]{3,2,1,0:T(8,128)S(1)}, f32[4,16,8,128]{3,2,1,0:T(8,128)S(1)}, u32[]{:S(2)}, u32[]{:S(2)}) collective-permute-start(f32[4,16,8,128]{3,2,1,0:T(8,128)S(1)} %get-tuple-element.39.refs_5_.refs_10_), channel_id=1, source_target_pairs={{0,2},{1,3},{2,0},{3,1},{4,6},{5,7},{6,4},{7,5},{8,10},{9,11},{10,... | collective-permute-start | bytes 786440 | tf_op jit(solution)/shard_map/ppermute | solution.py:265
  57.5 17.0 %collective-permute-start.5 = (f32[2,4,16,8,128]{4,3,2,1,0:T(8,128)S(1)}, f32[2,4,16,8,128]{4,3,2,1,0:T(8,128)S(1)}, u32[]{:S(2)}, u32[]{:S(2)}) collective-permute-start(f32[2,4,16,8,128]{4,3,2,1,0:T(8,128)S(1)} %f2o.1.refs_1_.refs_2_.refs_7_.refs_3_), channel_id=1, source_target_pairs={{0,255},{1,4},{2,253},{3,6},{4,1},{5,8},{6,3},{7,10},{8,5},{9,12},... | collective-permute-start | bytes 1572872 | tf_op jit(solution)/shard_map/ppermute | solution.py:277
  63.4 13.4 %collective-permute-start.9 = (f32[2,4,16,8,128]{4,3,2,1,0:T(8,128)S(1)}, f32[2,4,16,8,128]{4,3,2,1,0:T(8,128)S(1)}, u32[]{:S(2)}, u32[]{:S(2)}) collective-permute-start(f32[2,4,16,8,128]{4,3,2,1,0:T(8,128)S(1)} %f2i.1.refs_2_.refs_1_.refs_7_.refs_3_), channel_id=1, source_target_pairs={{0,1},{1,0},{2,3},{3,2},{4,5},{5,4},{6,7},{7,6},{8,9},{9,8},{10,11... | collective-permute-start | bytes 1572872 | tf_op jit(solution)/shard_map/ppermute | solution.py:262
  76.7 15.2 %collective-permute-start.8 = (f32[2,4,16,8,128]{4,3,2,1,0:T(8,128)S(1)}, f32[2,4,16,8,128]{4,3,2,1,0:T(8,128)S(1)}, u32[]{:S(2)}, u32[]{:S(2)}) collective-permute-start(f32[2,4,16,8,128]{4,3,2,1,0:T(8,128)S(1)} %f3o.1.refs_1_.refs_2_.refs_3_), channel_id=1, source_target_pairs={{0,255},{1,4},{2,253},{3,6},{4,1},{5,8},{6,3},{7,10},{8,5},{9,12},... | collective-permute-start | bytes 1572872 | tf_op jit(solution)/shard_map/ppermute | solution.py:277
  78.9 15.2 %collective-permute-start.11 = (f32[2,4,16,8,128]{4,3,2,1,0:T(8,128)S(1)}, f32[2,4,16,8,128]{4,3,2,1,0:T(8,128)S(1)}, u32[]{:S(2)}, u32[]{:S(2)}) collective-permute-start(f32[2,4,16,8,128]{4,3,2,1,0:T(8,128)S(1)} %f3i.1.refs_2_.refs_1_.refs_3_), channel_id=1, source_target_pairs={{0,1},{1,0},{2,3},{3,2},{4,5},{5,4},{6,7},{7,6},{8,9},{9,8},{10,11... | collective-permute-start | bytes 1572872 | tf_op jit(solution)/shard_map/ppermute | solution.py:262
  94.0 14.3 %collective-permute-start.10 = (f32[2,4,16,8,128]{4,3,2,1,0:T(8,128)S(1)}, f32[2,4,16,8,128]{4,3,2,1,0:T(8,128)S(1)}, u32[]{:S(2)}, u32[]{:S(2)}) collective-permute-start(f32[2,4,16,8,128]{4,3,2,1,0:T(8,128)S(1)} %get-tuple-element.40.refs_1_.refs_2_), channel_id=1, source_target_pairs={{0,255},{1,4},{2,253},{3,6},{4,1},{5,8},{6,3},{7,10},{8,5},{9,12},... | collective-permute-start | bytes 1572872 | tf_op jit(solution)/shard_map/ppermute | solution.py:277
  96.3 14.2 %collective-permute-start.13 = (f32[2,4,16,8,128]{4,3,2,1,0:T(8,128)S(1)}, f32[2,4,16,8,128]{4,3,2,1,0:T(8,128)S(1)}, u32[]{:S(2)}, u32[]{:S(2)}) collective-permute-start(f32[2,4,16,8,128]{4,3,2,1,0:T(8,128)S(1)} %get-tuple-element.41.refs_2_.refs_1_), channel_id=1, source_target_pairs={{0,1},{1,0},{2,3},{3,2},{4,5},{5,4},{6,7},{7,6},{8,9},{9,8},{10,11... | collective-permute-start | bytes 1572872 | tf_op jit(solution)/shard_map/ppermute | solution.py:262
  110.4 13.8 %collective-permute-start.12 = (f32[2,4,16,8,128]{4,3,2,1,0:T(8,128)S(1)}, f32[2,4,16,8,128]{4,3,2,1,0:T(8,128)S(1)}, u32[]{:S(2)}, u32[]{:S(2)}) collective-permute-start(f32[2,4,16,8,128]{4,3,2,1,0:T(8,128)S(1)} %get-tuple-element.43.refs_1_.refs_2_), channel_id=1, source_target_pairs={{0,255},{1,4},{2,253},{3,6},{4,1},{5,8},{6,3},{7,10},{8,5},{9,12},... | collective-permute-start | bytes 1572872 | tf_op jit(solution)/shard_map/ppermute | solution.py:277
  112.5 13.8 %collective-permute-start.15 = (f32[2,4,16,8,128]{4,3,2,1,0:T(8,128)S(1)}, f32[2,4,16,8,128]{4,3,2,1,0:T(8,128)S(1)}, u32[]{:S(2)}, u32[]{:S(2)}) collective-permute-start(f32[2,4,16,8,128]{4,3,2,1,0:T(8,128)S(1)} %get-tuple-element.45.refs_2_.refs_1_), channel_id=1, source_target_pairs={{0,1},{1,0},{2,3},{3,2},{4,5},{5,4},{6,7},{7,6},{8,9},{9,8},{10,11... | collective-permute-start | bytes 1572872 | tf_op jit(solution)/shard_map/ppermute | solution.py:262
  126.3 14.1 %collective-permute-start.14 = (f32[2,4,16,8,128]{4,3,2,1,0:T(8,128)S(1)}, f32[2,4,16,8,128]{4,3,2,1,0:T(8,128)S(1)}, u32[]{:S(2)}, u32[]{:S(2)}) collective-permute-start(f32[2,4,16,8,128]{4,3,2,1,0:T(8,128)S(1)} %get-tuple-element.47.refs_1_.refs_2_), channel_id=1, source_target_pairs={{0,255},{1,4},{2,253},{3,6},{4,1},{5,8},{6,3},{7,10},{8,5},{9,12},... | collective-permute-start | bytes 1572872 | tf_op jit(solution)/shard_map/ppermute | solution.py:277
  128.5 14.3 %collective-permute-start.16 = (f32[2,4,16,8,128]{4,3,2,1,0:T(8,128)S(1)}, f32[2,4,16,8,128]{4,3,2,1,0:T(8,128)S(1)}, u32[]{:S(2)}, u32[]{:S(2)}) collective-permute-start(f32[2,4,16,8,128]{4,3,2,1,0:T(8,128)S(1)} %get-tuple-element.49.refs_2_.refs_1_), channel_id=1, source_target_pairs={{0,1},{1,0},{2,3},{3,2},{4,5},{5,4},{6,7},{7,6},{8,9},{9,8},{10,11... | collective-permute-start | bytes 1572872 | tf_op jit(solution)/shard_map/ppermute | solution.py:262
  146.6 12.1 %collective-permute-start.17 = (f32[512,128]{1,0:T(8,128)S(1)}, f32[512,128]{1,0:T(8,128)S(1)}, u32[]{:S(2)}, u32[]{:S(2)}) collective-permute-start(f32[512,128]{1,0:T(8,128)S(1)} %get-tuple-element.53), channel_id=1, source_target_pairs={{0,2},{1,3},{2,0},{3,1},{4,6},{5,7},{6,4},{7,5},{8,10},{9,11},{10,... | collective-permute-start | bytes 786440 | tf_op jit(solution)/shard_map/ppermute | solution.py:265
  160.0 28.6 %all-to-all-start = ((f32[256,1,128]{2,1,0:T(1,128)}), f32[256,1,128]{2,1,0:T(1,128)S(1)}, u32[]{:S(2)}, u32[]{:S(2)}) async-start(f32[256,1,128]{2,1,0:T(1,128)} %bitcast.21), calls=%async_computation | async-start | bytes 262144 | tf_op jit(solution)/shard_map/all_to_all | solution.py:355
  175.7 3.2 %collective-permute-start.18 = (f32[256,128]{1,0:T(8,128)S(1)}, f32[256,128]{1,0:T(8,128)S(1)}, u32[]{:S(2)}, u32[]{:S(2)}) collective-permute-start(f32[256,128]{1,0:T(8,128)S(1)} %get-tuple-element.56), channel_id=1, source_target_pairs={{0,1},{1,0},{2,3},{3,2},{4,5},{5,4},{6,7},{7,6},{8,9},{9,8},{10,11... | collective-permute-start | bytes 393224 | tf_op jit(solution)/shard_map/ppermute | solution.py:262
